TPU v7x, 32 devices: a whole 2x2x4 slice. The times are simulated.
32 devices in a mesh: groups: 2 (over x), views: 16 (over z, y, core).
Axes of the slice: x: 2, y: 2, z: 4, core: 2. Of those that a mesh axis runs over, the one named last changes fastest.
Arguments:
- tokens: bfloat16 [32, 128, 1024], P(('groups', 'views')), parts along dimension 0, may hold values from -6 to 6
- in_gain: float32 [1024], replicated, may hold values from 0.7 to 6, as said below
- w_query: bfloat16 [1024, 1024], replicated, may hold values from -0.1875 to 0.1875
- w_key: bfloat16 [1024, 1024], replicated, may hold values from -0.1875 to 0.1875
- w_value: bfloat16 [1024, 1024], replicated, may hold values from -0.1875 to 0.1875
- w_out: bfloat16 [1024, 1024], replicated, may hold values from -0.1875 to 0.1875
- out_gain: float32 [1024], replicated, may hold values from 0.1 to 1.9
- covis_list: int32 [32, 12], P(('groups', 'views')), parts along dimension 0, may hold values from 0 to 15, as said below
- covis_count: int32 [32], P(('groups', 'views')), parts along dimension 0, may hold values from 2 to 12
Outputs:
- mixed: bfloat16 [32, 128, 1024], P(('groups', 'views')), parts along dimension 0
There are 2 independent parts, one for each index of `groups`. A program takes and returns all parts, laid end to end along the dimension named above; an argument that names none is the same for every part. Nothing has to cross between parts.
Inputs may be any that keep to these rules, and one draw needn't show every extreme that they name: `covis_list`: row v lists 12 distinct view ids w, each with w - v modulo 16 among -6 to -1 and 1 to 6; only the first covis_count[v] entries are covisible views, the others are not used. `in_gain`: positive gains.
All inputs are finite; a program needn't handle non-finite values.
Results may differ from a plain program's by a relative error of at most 0.0085.
The roundings to bfloat16 on the way count: a program that leaves them out, or rounds other values in their place, can miss the bound.
Values may be sent and summed in bfloat16 or wider, within the bound.
A program may use at most 128 MiB of HBM per device.

v0:
```python
import jax
import jax.numpy as jnp
from jax import lax
from jax.sharding import PartitionSpec as P

HEADS = 16
HEAD_DIM = 64
REACH = 6


def from_behind(block, axis, distance):
    devices = range(lax.axis_size(axis))
    route = [((i - distance) % len(devices), i) for i in devices]
    return lax.ppermute(block, axis, route)


def rms_scale(values, gain):
    mean_sq = jnp.mean(values * values, axis=-1, keepdims=True)
    return values * lax.rsqrt(mean_sq + 1e-06) * gain


def attend_block(query3, key_flat, value_flat):
    tok_rows = query3.shape[0]
    key3 = key_flat.reshape(-1, HEADS, HEAD_DIM)
    value3 = value_flat.reshape(-1, HEADS, HEAD_DIM)
    scores = jnp.einsum(
        "qhd,khd->qhk", query3, key3, preferred_element_type=jnp.float32
    ) * HEAD_DIM ** (-0.5)
    peak = jnp.max(scores, axis=-1)
    weights = jnp.exp(scores - peak[..., None])
    total = jnp.sum(weights, axis=-1)
    numer = jnp.einsum(
        "qhk,khd->qhd", weights.astype(jnp.bfloat16), value3, preferred_element_type=jnp.float32
    )
    return (numer.reshape(tok_rows, HEADS * HEAD_DIM), peak, total)


def combine(state, piece, flag):
    numer, peak, total = state
    other_numer, other_peak, other_total = piece
    other_peak = jnp.where(flag, other_peak, -jnp.inf)
    newest = jnp.maximum(peak, other_peak)
    keep_old = jnp.exp(peak - newest)
    keep_new = jnp.where(flag, jnp.exp(other_peak - newest), 0.0)
    tok_rows = numer.shape[0]
    numer = (
        numer.reshape(tok_rows, HEADS, HEAD_DIM) * keep_old[..., None]
        + other_numer.reshape(tok_rows, HEADS, HEAD_DIM) * keep_new[..., None]
    ).reshape(tok_rows, HEADS * HEAD_DIM)
    total = total * keep_old + other_total * keep_new
    return (numer, newest, total)


def on_device(tokens, in_gain, w_query, w_key, w_value, w_out, out_gain, covis_list, covis_count):
    view_count = lax.axis_size("views")
    own_view = lax.axis_index("views")
    source = tokens[0]
    tok_rows = source.shape[0]
    width = source.shape[1]
    normed = rms_scale(source.astype(jnp.float32), in_gain).astype(jnp.bfloat16)
    query = jnp.dot(normed, w_query, preferred_element_type=jnp.float32).astype(jnp.bfloat16)
    key_own = jnp.dot(normed, w_key, preferred_element_type=jnp.float32).astype(jnp.bfloat16)
    value_own = jnp.dot(normed, w_value, preferred_element_type=jnp.float32).astype(jnp.bfloat16)
    query3 = query.reshape(tok_rows, HEADS, HEAD_DIM)
    listed_row = covis_list[0]
    valid = jnp.arange(listed_row.shape[0], dtype=jnp.int32) < covis_count[0]

    def flag_for(offset):
        target = (own_view + offset) % view_count
        return jnp.any((listed_row == target) & valid)

    state = attend_block(query3, key_own, value_own)
    upward = (key_own, value_own)
    downward = (key_own, value_own)
    for step in range(1, REACH + 1):
        upward = from_behind((upward[0], upward[1]), "views", 1)
        state = combine(state, attend_block(query3, upward[0], upward[1]), flag_for(-step))
        downward = from_behind((downward[0], downward[1]), "views", -1)
        state = combine(state, attend_block(query3, downward[0], downward[1]), flag_for(step))
    numer, peak, total = state
    attended = numer.reshape(tok_rows, HEADS, HEAD_DIM) / total[..., None]
    head_normed = (
        rms_scale(attended, out_gain.reshape(HEADS, HEAD_DIM))
        .astype(jnp.bfloat16)
        .reshape(tok_rows, width)
    )
    update = jnp.dot(head_normed, w_out, preferred_element_type=jnp.float32)
    return (source.astype(jnp.float32) + update).astype(jnp.bfloat16)[None]


def solution(mesh):
    in_specs = (
        P(("groups", "views"), None, None),
        P(),
        P(),
        P(),
        P(),
        P(),
        P(),
        P(("groups", "views"), None),
        P(("groups", "views")),
    )
    out_specs = P(("groups", "views"), None, None)
    return jax.shard_map(
        on_device, mesh=mesh, in_specs=in_specs, out_specs=out_specs, check_vma=False
    )
```

profile of v0, /device:TPU:1, one launch (start us, length us, event | category | flops | bytes accessed | tf_op | source)
XLA Modules:
  0.0 155.2 jit_solution(14820396399054723734)
XLA Ops:
  1.7 2.1 %convolution_convert_fusion.1 = bf16[128,1024]{1,0:T(8,128)(2,1)} fusion(bf16[1024,1024]{1,0:T(8,128)(2,1)S(1)} %copy-done, bf16[1,128,1024]{2,1,0:T(8,128)(2,1)} %param.9, f32[1024]{0:T(1024)} %param.10, f32[128]{0:T(128)S(1)} %add_rsqrt_fusion.1), kind=kOutput, calls=%fused_computation.78 | convolution fusion | flops 269090816 | bytes 2626048 | tf_op jit(solution)/shard_map/dot_general | solution.py:62
  3.8 2.6 %collective-permute-start = (bf16[128,1024]{1,0:T(8,128)(2,1)}, bf16[128,1024]{1,0:T(8,128)(2,1)}, u32[]{:S(2)}, u32[]{:S(2)}) collective-permute-start(bf16[128,1024]{1,0:T(8,128)(2,1)} %convolution_convert_fusion.1), channel_id=1, source_target_pairs={{15,0},{0,1},{1,2},{2,3},{3,4},{4,5},{5,6},{6,7},{7,8},{8,9},{9,10... | collective-permute-start | bytes 786440 | tf_op jit(solution)/shard_map/ppermute | solution.py:14
  7.7 2.9 %collective-permute-start.3 = (bf16[128,1024]{1,0:T(8,128)(2,1)}, bf16[128,1024]{1,0:T(8,128)(2,1)}, u32[]{:S(2)}, u32[]{:S(2)}) collective-permute-start(bf16[128,1024]{1,0:T(8,128)(2,1)} %convolution_convert_fusion.2), channel_id=1, source_target_pairs={{1,0},{2,1},{3,2},{4,3},{5,4},{6,5},{7,6},{8,7},{9,8},{10,9},{11,1... | collective-permute-start | bytes 786440 | tf_op jit(solution)/shard_map/ppermute | solution.py:14
  10.6 1.8 %copy.63 = bf16[128,1024]{0,1:T(8,128)(2,1)} copy(bf16[128,1024]{1,0:T(8,128)(2,1)} %convolution_convert_fusion.1) | data formatting | bytes 524288 | tf_op jit(solution)/shard_map/convert_element_type | solution.py:62
  14.8 2.1 %convolution_convert_fusion = bf16[128,1024]{1,0:T(8,128)(2,1)S(1)} fusion(bf16[1024,1024]{1,0:T(8,128)(2,1)} %param.11, bf16[1,128,1024]{2,1,0:T(8,128)(2,1)S(1)} %copy-done.15, f32[1024]{0:T(1024)S(1)} %copy-done.31, f32[128]{0:T(128)S(1)} %add_rsqrt_fusion.1), kind=kOutput, calls=%fused_computation.77 | convolution fusion | flops 269090816 | bytes 2626048 | tf_op jit(solution)/shard_map/dot_general | solution.py:61
  20.0 1.8 %copy.66 = bf16[128,1024]{0,1:T(8,128)(2,1)} copy(bf16[128,1024]{1,0:T(8,128)(2,1)} %collective-permute-done) | data formatting | bytes 524288 | tf_op jit(solution)/shard_map/ppermute | solution.py:14
  21.8 2.3 %fusion.138 = (f32[128,16]{0,1:T(8,128)S(1)}, f32[128,16,128]{0,2,1:T(8,128)}) fusion(bf16[128,16,64]{0,2,1:T(8,128)(2,1)} %bitcast.290, bf16[128,16,64]{0,2,1:T(8,128)(2,1)S(1)} %bitcast.259), kind=kOutput, calls=%fused_computation.218 | convolution fusion | flops 34076672 | bytes 1581056 | tf_op jit(solution)/shard_map/qhd,khd->qhk/dot_general | solution.py:26
  24.1 4.4 %collective-permute-start.6 = (bf16[128,1024]{1,0:T(8,128)(2,1)}, bf16[128,1024]{1,0:T(8,128)(2,1)}, u32[]{:S(2)}, u32[]{:S(2)}) collective-permute-start(bf16[128,1024]{1,0:T(8,128)(2,1)} %collective-permute-done.2), channel_id=1, source_target_pairs={{1,0},{2,1},{3,2},{4,3},{5,4},{6,5},{7,6},{8,7},{9,8},{10,9},{11,1... | collective-permute-start | bytes 786440 | tf_op jit(solution)/shard_map/ppermute | solution.py:14
  30.3 1.8 %copy.70 = bf16[128,1024]{0,1:T(8,128)(2,1)} copy(bf16[128,1024]{1,0:T(8,128)(2,1)} %collective-permute-done.3) | data formatting | bytes 524288 | tf_op jit(solution)/shard_map/ppermute | solution.py:14
  32.1 4.5 %collective-permute-start.7 = (bf16[128,1024]{1,0:T(8,128)(2,1)}, bf16[128,1024]{1,0:T(8,128)(2,1)}, u32[]{:S(2)}, u32[]{:S(2)}) collective-permute-start(bf16[128,1024]{1,0:T(8,128)(2,1)} %collective-permute-done.3), channel_id=1, source_target_pairs={{1,0},{2,1},{3,2},{4,3},{5,4},{6,5},{7,6},{8,7},{9,8},{10,9},{11,1... | collective-permute-start | bytes 786440 | tf_op jit(solution)/shard_map/ppermute | solution.py:14
  38.2 1.8 %copy.67 = bf16[128,1024]{0,1:T(8,128)(2,1)} copy(bf16[128,1024]{1,0:T(8,128)(2,1)} %collective-permute-done.1) | data formatting | bytes 524288 | tf_op jit(solution)/shard_map/ppermute | solution.py:14
  40.0 2.3 %fusion.137 = (f32[128,16]{0,1:T(8,128)S(1)}, f32[128,16,128]{0,2,1:T(8,128)}) fusion(bf16[128,16,64]{0,2,1:T(8,128)(2,1)} %bitcast.287, bf16[128,16,64]{0,2,1:T(8,128)(2,1)S(1)} %bitcast.260), kind=kOutput, calls=%fused_computation.217 | convolution fusion | flops 34076672 | bytes 1581056 | tf_op jit(solution)/shard_map/qhd,khd->qhk/dot_general | solution.py:26
  44.1 2.3 %fusion.136 = (f32[128,16]{0,1:T(8,128)S(1)}, f32[128,16,128]{0,2,1:T(8,128)}) fusion(bf16[128,16,64]{0,2,1:T(8,128)(2,1)} %bitcast.291, bf16[128,16,64]{0,2,1:T(8,128)(2,1)S(1)} %bitcast.261), kind=kOutput, calls=%fused_computation.216 | convolution fusion | flops 34076672 | bytes 1581056 | tf_op jit(solution)/shard_map/qhd,khd->qhk/dot_general | solution.py:26
  50.5 4.5 %collective-permute-start.11 = (bf16[128,1024]{1,0:T(8,128)(2,1)}, bf16[128,1024]{1,0:T(8,128)(2,1)}, u32[]{:S(2)}, u32[]{:S(2)}) collective-permute-start(bf16[128,1024]{1,0:T(8,128)(2,1)} %collective-permute-done.7), channel_id=1, source_target_pairs={{1,0},{2,1},{3,2},{4,3},{5,4},{6,5},{7,6},{8,7},{9,8},{10,9},{11,1... | collective-permute-start | bytes 786440 | tf_op jit(solution)/shard_map/ppermute | solution.py:14
  55.0 1.9 %fusion.56 = (f32[128,16]{0,1:T(8,128)S(1)}, f32[128,16]{0,1:T(8,128)S(1)}) fusion(f32[128,16,128]{0,2,1:T(8,128)} %get-tuple-element.68, f32[128,16]{0,1:T(8,128)S(1)} %get-tuple-element.67, f32[128,16,128]{0,2,1:T(8,128)} %get-tuple-element.66, f32[128,16]{0,1:T(8,128)S(1)} %get-tuple-element.65), kind=kLoop, calls=%fused_computation.99 | loop fusion | flops 1044480 | bytes 2129920 | tf_op jit(solution)/shard_map/reduce_sum | solution.py:31
  58.7 2.3 %fusion.135 = (f32[128,16]{0,1:T(8,128)S(1)}, f32[128,16,128]{0,2,1:T(8,128)}) fusion(bf16[128,16,64]{0,2,1:T(8,128)(2,1)} %bitcast.284, bf16[128,16,64]{0,2,1:T(8,128)(2,1)S(1)} %bitcast.262), kind=kOutput, calls=%fused_computation.215 | convolution fusion | flops 34076672 | bytes 1581056 | tf_op jit(solution)/shard_map/qhd,khd->qhk/dot_general | solution.py:26
  62.8 2.3 %fusion.134 = (f32[128,16]{0,1:T(8,128)S(1)}, f32[128,16,128]{0,2,1:T(8,128)}) fusion(bf16[128,16,64]{0,2,1:T(8,128)(2,1)} %bitcast.292, bf16[128,16,64]{0,2,1:T(8,128)(2,1)S(1)} %bitcast.263), kind=kOutput, calls=%fused_computation.214 | convolution fusion | flops 34076672 | bytes 1581056 | tf_op jit(solution)/shard_map/qhd,khd->qhk/dot_general | solution.py:26
  69.2 4.5 %collective-permute-start.15 = (bf16[128,1024]{1,0:T(8,128)(2,1)}, bf16[128,1024]{1,0:T(8,128)(2,1)}, u32[]{:S(2)}, u32[]{:S(2)}) collective-permute-start(bf16[128,1024]{1,0:T(8,128)(2,1)} %collective-permute-done.11), channel_id=1, source_target_pairs={{1,0},{2,1},{3,2},{4,3},{5,4},{6,5},{7,6},{8,7},{9,8},{10,9},{11,1... | collective-permute-start | bytes 786440 | tf_op jit(solution)/shard_map/ppermute | solution.py:14
  73.6 2.5 %fusion.60 = (f32[128,16]{0,1:T(8,128)S(1)}, f32[128,16]{0,1:T(8,128)}) fusion(f32[128,16,128]{0,2,1:T(8,128)} %get-tuple-element.64, f32[128,16]{0,1:T(8,128)S(1)} %get-tuple-element.63, f32[128,16,128]{0,2,1:T(8,128)} %get-tuple-element.62, f32[128,16]{0,1:T(8,128)S(1)} %get-tuple-element.61), kind=kLoop, calls=%fused_computation.103 | loop fusion | flops 1044480 | bytes 2129920 | tf_op jit(solution)/shard_map/reduce_sum | solution.py:31
  77.9 2.3 %fusion.133 = (f32[128,16]{0,1:T(8,128)S(1)}, f32[128,16,128]{0,2,1:T(8,128)}) fusion(bf16[128,16,64]{0,2,1:T(8,128)(2,1)} %bitcast.285, bf16[128,16,64]{0,2,1:T(8,128)(2,1)S(1)} %bitcast.264), kind=kOutput, calls=%fused_computation.213 | convolution fusion | flops 34076672 | bytes 1581056 | tf_op jit(solution)/shard_map/qhd,khd->qhk/dot_general | solution.py:26
  82.0 2.3 %fusion.132 = (f32[128,16]{0,1:T(8,128)S(1)}, f32[128,16,128]{0,2,1:T(8,128)}) fusion(bf16[128,16,64]{0,2,1:T(8,128)(2,1)} %bitcast.293, bf16[128,16,64]{0,2,1:T(8,128)(2,1)S(1)} %bitcast.265), kind=kOutput, calls=%fused_computation.212 | convolution fusion | flops 34076672 | bytes 1581056 | tf_op jit(solution)/shard_map/qhd,khd->qhk/dot_general | solution.py:26
  86.6 1.8 %copy.88 = bf16[128,1024]{0,1:T(8,128)(2,1)} copy(bf16[128,1024]{1,0:T(8,128)(2,1)} %collective-permute-done.15) | data formatting | bytes 524288 | tf_op jit(solution)/shard_map/ppermute | solution.py:14
  88.4 4.5 %collective-permute-start.19 = (bf16[128,1024]{1,0:T(8,128)(2,1)}, bf16[128,1024]{1,0:T(8,128)(2,1)}, u32[]{:S(2)}, u32[]{:S(2)}) collective-permute-start(bf16[128,1024]{1,0:T(8,128)(2,1)} %collective-permute-done.15), channel_id=1, source_target_pairs={{1,0},{2,1},{3,2},{4,3},{5,4},{6,5},{7,6},{8,7},{9,8},{10,9},{11,1... | collective-permute-start | bytes 786440 | tf_op jit(solution)/shard_map/ppermute | solution.py:14
  92.9 2.5 %fusion.64 = (f32[128,16]{0,1:T(8,128)}, f32[128,16]{0,1:T(8,128)}) fusion(f32[128,16,128]{0,2,1:T(8,128)} %get-tuple-element.60, f32[128,16]{0,1:T(8,128)S(1)} %get-tuple-element.59, f32[128,16,128]{0,2,1:T(8,128)} %get-tuple-element.58, f32[128,16]{0,1:T(8,128)S(1)} %get-tuple-element.57), kind=kLoop, calls=%fused_computation.107 | loop fusion | flops 1044480 | bytes 2129920 | tf_op jit(solution)/shard_map/reduce_sum | solution.py:31
  95.4 1.8 %copy.85 = bf16[128,1024]{0,1:T(8,128)(2,1)} copy(bf16[128,1024]{1,0:T(8,128)(2,1)} %collective-permute-done.13) | data formatting | bytes 524288 | tf_op jit(solution)/shard_map/ppermute | solution.py:14
  97.2 2.3 %fusion.131 = (f32[128,16]{0,1:T(8,128)S(1)}, f32[128,16,128]{0,2,1:T(8,128)}) fusion(bf16[128,16,64]{0,2,1:T(8,128)(2,1)} %bitcast.286, bf16[128,16,64]{0,2,1:T(8,128)(2,1)S(1)} %bitcast.266), kind=kOutput, calls=%fused_computation.211 | convolution fusion | flops 34076672 | bytes 1581056 | tf_op jit(solution)/shard_map/qhd,khd->qhk/dot_general | solution.py:26
  101.3 2.3 %fusion.129 = (f32[128,16]{0,1:T(8,128)S(1)}, f32[128,16,128]{0,2,1:T(8,128)}) fusion(bf16[128,16,64]{0,2,1:T(8,128)(2,1)} %bitcast.294, bf16[128,16,64]{0,2,1:T(8,128)(2,1)S(1)} %bitcast.267), kind=kOutput, calls=%fused_computation.209 | convolution fusion | flops 34076672 | bytes 1581056 | tf_op jit(solution)/shard_map/qhd,khd->qhk/dot_general | solution.py:26
  110.1 4.4 %collective-permute-start.23 = (bf16[128,1024]{1,0:T(8,128)(2,1)}, bf16[128,1024]{1,0:T(8,128)(2,1)}, u32[]{:S(2)}, u32[]{:S(2)}) collective-permute-start(bf16[128,1024]{1,0:T(8,128)(2,1)} %collective-permute-done.19), channel_id=1, source_target_pairs={{1,0},{2,1},{3,2},{4,3},{5,4},{6,5},{7,6},{8,7},{9,8},{10,9},{11,1... | collective-permute-start | bytes 786440 | tf_op jit(solution)/shard_map/ppermute | solution.py:14
  116.3 6.9 %select_maximum_fusion.1 = (f32[128,16]{0,1:T(8,128)}, f32[128,16]{0,1:T(8,128)}, f32[128,16]{0,1:T(8,128)}, f32[128,16]{0,1:T(8,128)}, f32[128,16]{0,1:T(8,128)}) fusion(f32[128,16]{0,1:T(8,128)S(1)} %get-tuple-element.51, pred[]{:T(512)} %get-tuple-element.6, f32[128,16]{0,1:T(8,128)S(1)} %get-tuple-element.53, pred[]{:T(512)} %get-tuple-element.7, ...), kind=kLoop, calls=%fused_computation.171 | loop fusion | flops 40960 | bytes 131082 | tf_op jit(solution)/shard_map/max | solution.py:42
  125.0 2.4 %fusion.128 = (f32[128,16]{0,1:T(8,128)S(1)}, f32[128,16,128]{0,2,1:T(8,128)}) fusion(bf16[128,16,64]{0,2,1:T(8,128)(2,1)} %bitcast.289, bf16[128,16,64]{0,2,1:T(8,128)(2,1)S(1)} %bitcast.269), kind=kOutput, calls=%fused_computation.208 | convolution fusion | flops 34076672 | bytes 1581056 | tf_op jit(solution)/shard_map/qhd,khd->qhk/dot_general | solution.py:26
  132.4 8.4 %multiply_add_fusion = (f32[128,16]{0,1:T(8,128)}, f32[128,16]{0,1:T(8,128)}, f32[128,16]{0,1:T(8,128)}, f32[128,16]{0,1:T(8,128)S(1)}, f32[128,16]{0,1:T(8,128)...) fusion(f32[128,16]{0,1:T(8,128)S(1)} %fusion.76, ...), kind=kLoop, calls=%fused_computation.147 | loop fusion | flops 186368 | bytes 458764 | tf_op jit(solution)/shard_map/add | solution.py:50
  151.7 2.0 %multiply_reduce_fusion = (f32[128,16]{0,1:T(8,128)S(1)}, f32[128,16,64]{0,2,1:T(8,128)S(1)}) fusion(f32[128,16]{0,1:T(8,128)S(1)} %copy-done.44, f32[128,16,64]{0,2,1:T(8,128)} %fusion.49, f32[128,16]{0,1:T(8,128)S(1)} %copy-done.46, f32[128,16,64]{0,2,1:T(8,128)} %fusion.42, f32[128,16]{0,1:T(8,128)S(1)} %copy-done.45, ...), kind=kOutput, calls=%fused_computation.127 | convolution fusion | flops 34994176 | bytes 2924544 | tf_op jit(solution)/shard_map/qhk,khd->qhd/dot_general | solution.py:32
  (186 shorter events, 59.4 us)
Async XLA Ops:
  0.0 6.4 %copy-start.31 = (f32[1024]{0:T(1024)S(1)}, f32[1024]{0:T(1024)}, u32[]{:S(2)}) copy-start(f32[1024]{0:T(1024)} %param.10) | copy-start | bytes 12292
  3.8 20.3 %collective-permute-start.2 = (bf16[128,1024]{1,0:T(8,128)(2,1)}, bf16[128,1024]{1,0:T(8,128)(2,1)}, u32[]{:S(2)}, u32[]{:S(2)}) collective-permute-start(bf16[128,1024]{1,0:T(8,128)(2,1)} %convolution_convert_fusion.1), channel_id=1, source_target_pairs={{1,0},{2,1},{3,2},{4,3},{5,4},{6,5},{7,6},{8,7},{9,8},{10,9},{11,1... | collective-permute-start | bytes 786440 | tf_op jit(solution)/shard_map/ppermute | solution.py:14
  3.8 16.2 %collective-permute-start = (bf16[128,1024]{1,0:T(8,128)(2,1)}, bf16[128,1024]{1,0:T(8,128)(2,1)}, u32[]{:S(2)}, u32[]{:S(2)}) collective-permute-start(bf16[128,1024]{1,0:T(8,128)(2,1)} %convolution_convert_fusion.1), channel_id=1, source_target_pairs={{15,0},{0,1},{1,2},{2,3},{3,4},{4,5},{5,6},{6,7},{7,8},{8,9},{9,10... | collective-permute-start | bytes 786440 | tf_op jit(solution)/shard_map/ppermute | solution.py:14
  7.7 22.7 %collective-permute-start.3 = (bf16[128,1024]{1,0:T(8,128)(2,1)}, bf16[128,1024]{1,0:T(8,128)(2,1)}, u32[]{:S(2)}, u32[]{:S(2)}) collective-permute-start(bf16[128,1024]{1,0:T(8,128)(2,1)} %convolution_convert_fusion.2), channel_id=1, source_target_pairs={{1,0},{2,1},{3,2},{4,3},{5,4},{6,5},{7,6},{8,7},{9,8},{10,9},{11,1... | collective-permute-start | bytes 786440 | tf_op jit(solution)/shard_map/ppermute | solution.py:14
  10.5 27.7 %collective-permute-start.1 = (bf16[128,1024]{1,0:T(8,128)(2,1)}, bf16[128,1024]{1,0:T(8,128)(2,1)}, u32[]{:S(2)}, u32[]{:S(2)}) collective-permute-start(bf16[128,1024]{1,0:T(8,128)(2,1)} %convolution_convert_fusion.2), channel_id=1, source_target_pairs={{15,0},{0,1},{1,2},{2,3},{3,4},{4,5},{5,6},{6,7},{7,8},{8,9},{9,10... | collective-permute-start | bytes 786440 | tf_op jit(solution)/shard_map/ppermute | solution.py:14
  10.5 6.6 %copy-start.47 = (f32[1024]{0:T(1024)S(1)}, f32[1024]{0:T(1024)}, u32[]{:S(2)}) copy-start(f32[1024]{0:T(1024)} %param.15) | copy-start | bytes 12292
  10.5 7.2 %copy-start.48 = (s32[1,12]{1,0:T(1,128)S(1)}, s32[1,12]{1,0:T(1,128)}, u32[]{:S(2)}) copy-start(s32[1,12]{1,0:T(1,128)} %param.16) | copy-start | bytes 148
  24.1 18.2 %collective-permute-start.4 = (bf16[128,1024]{1,0:T(8,128)(2,1)}, bf16[128,1024]{1,0:T(8,128)(2,1)}, u32[]{:S(2)}, u32[]{:S(2)}) collective-permute-start(bf16[128,1024]{1,0:T(8,128)(2,1)} %collective-permute-done), channel_id=1, source_target_pairs={{15,0},{0,1},{1,2},{2,3},{3,4},{4,5},{5,6},{6,7},{7,8},{8,9},{9,10... | collective-permute-start | bytes 786440 | tf_op jit(solution)/shard_map/ppermute | solution.py:14
  24.1 22.3 %collective-permute-start.6 = (bf16[128,1024]{1,0:T(8,128)(2,1)}, bf16[128,1024]{1,0:T(8,128)(2,1)}, u32[]{:S(2)}, u32[]{:S(2)}) collective-permute-start(bf16[128,1024]{1,0:T(8,128)(2,1)} %collective-permute-done.2), channel_id=1, source_target_pairs={{1,0},{2,1},{3,2},{4,3},{5,4},{6,5},{7,6},{8,7},{9,8},{10,9},{11,1... | collective-permute-start | bytes 786440 | tf_op jit(solution)/shard_map/ppermute | solution.py:14
  32.1 16.6 %collective-permute-start.7 = (bf16[128,1024]{1,0:T(8,128)(2,1)}, bf16[128,1024]{1,0:T(8,128)(2,1)}, u32[]{:S(2)}, u32[]{:S(2)}) collective-permute-start(bf16[128,1024]{1,0:T(8,128)(2,1)} %collective-permute-done.3), channel_id=1, source_target_pairs={{1,0},{2,1},{3,2},{4,3},{5,4},{6,5},{7,6},{8,7},{9,8},{10,9},{11,1... | collective-permute-start | bytes 786440 | tf_op jit(solution)/shard_map/ppermute | solution.py:14
  40.0 16.9 %collective-permute-start.5 = (bf16[128,1024]{1,0:T(8,128)(2,1)}, bf16[128,1024]{1,0:T(8,128)(2,1)}, u32[]{:S(2)}, u32[]{:S(2)}) collective-permute-start(bf16[128,1024]{1,0:T(8,128)(2,1)} %collective-permute-done.1), channel_id=1, source_target_pairs={{15,0},{0,1},{1,2},{2,3},{3,4},{4,5},{5,6},{6,7},{7,8},{8,9},{9,10... | collective-permute-start | bytes 786440 | tf_op jit(solution)/shard_map/ppermute | solution.py:14
  46.4 14.6 %collective-permute-start.8 = (bf16[128,1024]{1,0:T(8,128)(2,1)}, bf16[128,1024]{1,0:T(8,128)(2,1)}, u32[]{:S(2)}, u32[]{:S(2)}) collective-permute-start(bf16[128,1024]{1,0:T(8,128)(2,1)} %collective-permute-done.4), channel_id=1, source_target_pairs={{15,0},{0,1},{1,2},{2,3},{3,4},{4,5},{5,6},{6,7},{7,8},{8,9},{9,10... | collective-permute-start | bytes 786440 | tf_op jit(solution)/shard_map/ppermute | solution.py:14
  46.4 18.6 %collective-permute-start.10 = (bf16[128,1024]{1,0:T(8,128)(2,1)}, bf16[128,1024]{1,0:T(8,128)(2,1)}, u32[]{:S(2)}, u32[]{:S(2)}) collective-permute-start(bf16[128,1024]{1,0:T(8,128)(2,1)} %collective-permute-done.6), channel_id=1, source_target_pairs={{1,0},{2,1},{3,2},{4,3},{5,4},{6,5},{7,6},{8,7},{9,8},{10,9},{11,1... | collective-permute-start | bytes 786440 | tf_op jit(solution)/shard_map/ppermute | solution.py:14
  50.5 16.9 %collective-permute-start.11 = (bf16[128,1024]{1,0:T(8,128)(2,1)}, bf16[128,1024]{1,0:T(8,128)(2,1)}, u32[]{:S(2)}, u32[]{:S(2)}) collective-permute-start(bf16[128,1024]{1,0:T(8,128)(2,1)} %collective-permute-done.7), channel_id=1, source_target_pairs={{1,0},{2,1},{3,2},{4,3},{5,4},{6,5},{7,6},{8,7},{9,8},{10,9},{11,1... | collective-permute-start | bytes 786440 | tf_op jit(solution)/shard_map/ppermute | solution.py:14
  58.7 17.4 %collective-permute-start.9 = (bf16[128,1024]{1,0:T(8,128)(2,1)}, bf16[128,1024]{1,0:T(8,128)(2,1)}, u32[]{:S(2)}, u32[]{:S(2)}) collective-permute-start(bf16[128,1024]{1,0:T(8,128)(2,1)} %collective-permute-done.5), channel_id=1, source_target_pairs={{15,0},{0,1},{1,2},{2,3},{3,4},{4,5},{5,6},{6,7},{7,8},{8,9},{9,10... | collective-permute-start | bytes 786440 | tf_op jit(solution)/shard_map/ppermute | solution.py:14
  65.1 15.2 %collective-permute-start.12 = (bf16[128,1024]{1,0:T(8,128)(2,1)}, bf16[128,1024]{1,0:T(8,128)(2,1)}, u32[]{:S(2)}, u32[]{:S(2)}) collective-permute-start(bf16[128,1024]{1,0:T(8,128)(2,1)} %collective-permute-done.8), channel_id=1, source_target_pairs={{15,0},{0,1},{1,2},{2,3},{3,4},{4,5},{5,6},{6,7},{7,8},{8,9},{9,10... | collective-permute-start | bytes 786440 | tf_op jit(solution)/shard_map/ppermute | solution.py:14
  65.1 19.3 %collective-permute-start.14 = (bf16[128,1024]{1,0:T(8,128)(2,1)}, bf16[128,1024]{1,0:T(8,128)(2,1)}, u32[]{:S(2)}, u32[]{:S(2)}) collective-permute-start(bf16[128,1024]{1,0:T(8,128)(2,1)} %collective-permute-done.10), channel_id=1, source_target_pairs={{1,0},{2,1},{3,2},{4,3},{5,4},{6,5},{7,6},{8,7},{9,8},{10,9},{11,1... | collective-permute-start | bytes 786440 | tf_op jit(solution)/shard_map/ppermute | solution.py:14
  69.2 17.5 %collective-permute-start.15 = (bf16[128,1024]{1,0:T(8,128)(2,1)}, bf16[128,1024]{1,0:T(8,128)(2,1)}, u32[]{:S(2)}, u32[]{:S(2)}) collective-permute-start(bf16[128,1024]{1,0:T(8,128)(2,1)} %collective-permute-done.11), channel_id=1, source_target_pairs={{1,0},{2,1},{3,2},{4,3},{5,4},{6,5},{7,6},{8,7},{9,8},{10,9},{11,1... | collective-permute-start | bytes 786440 | tf_op jit(solution)/shard_map/ppermute | solution.py:14
  77.9 17.5 %collective-permute-start.13 = (bf16[128,1024]{1,0:T(8,128)(2,1)}, bf16[128,1024]{1,0:T(8,128)(2,1)}, u32[]{:S(2)}, u32[]{:S(2)}) collective-permute-start(bf16[128,1024]{1,0:T(8,128)(2,1)} %collective-permute-done.9), channel_id=1, source_target_pairs={{15,0},{0,1},{1,2},{2,3},{3,4},{4,5},{5,6},{6,7},{7,8},{8,9},{9,10... | collective-permute-start | bytes 786440 | tf_op jit(solution)/shard_map/ppermute | solution.py:14
  84.3 19.2 %collective-permute-start.16 = (bf16[128,1024]{1,0:T(8,128)(2,1)}, bf16[128,1024]{1,0:T(8,128)(2,1)}, u32[]{:S(2)}, u32[]{:S(2)}) collective-permute-start(bf16[128,1024]{1,0:T(8,128)(2,1)} %collective-permute-done.12), channel_id=1, source_target_pairs={{15,0},{0,1},{1,2},{2,3},{3,4},{4,5},{5,6},{6,7},{7,8},{8,9},{9,10... | collective-permute-start | bytes 786440 | tf_op jit(solution)/shard_map/ppermute | solution.py:14
  84.3 15.2 %collective-permute-start.18 = (bf16[128,1024]{1,0:T(8,128)(2,1)}, bf16[128,1024]{1,0:T(8,128)(2,1)}, u32[]{:S(2)}, u32[]{:S(2)}) collective-permute-start(bf16[128,1024]{1,0:T(8,128)(2,1)} %collective-permute-done.14), channel_id=1, source_target_pairs={{1,0},{2,1},{3,2},{4,3},{5,4},{6,5},{7,6},{8,7},{9,8},{10,9},{11,1... | collective-permute-start | bytes 786440 | tf_op jit(solution)/shard_map/ppermute | solution.py:14
  88.4 19.9 %collective-permute-start.19 = (bf16[128,1024]{1,0:T(8,128)(2,1)}, bf16[128,1024]{1,0:T(8,128)(2,1)}, u32[]{:S(2)}, u32[]{:S(2)}) collective-permute-start(bf16[128,1024]{1,0:T(8,128)(2,1)} %collective-permute-done.15), channel_id=1, source_target_pairs={{1,0},{2,1},{3,2},{4,3},{5,4},{6,5},{7,6},{8,7},{9,8},{10,9},{11,1... | collective-permute-start | bytes 786440 | tf_op jit(solution)/shard_map/ppermute | solution.py:14
  97.2 17.3 %collective-permute-start.17 = (bf16[128,1024]{1,0:T(8,128)(2,1)}, bf16[128,1024]{1,0:T(8,128)(2,1)}, u32[]{:S(2)}, u32[]{:S(2)}) collective-permute-start(bf16[128,1024]{1,0:T(8,128)(2,1)} %collective-permute-done.13), channel_id=1, source_target_pairs={{15,0},{0,1},{1,2},{2,3},{3,4},{4,5},{5,6},{6,7},{7,8},{8,9},{9,10... | collective-permute-start | bytes 786440 | tf_op jit(solution)/shard_map/ppermute | solution.py:14
  106.8 16.4 %collective-permute-start.20 = (bf16[128,1024]{1,0:T(8,128)(2,1)}, bf16[128,1024]{1,0:T(8,128)(2,1)}, u32[]{:S(2)}, u32[]{:S(2)}) collective-permute-start(bf16[128,1024]{1,0:T(8,128)(2,1)} %collective-permute-done.16), channel_id=1, source_target_pairs={{15,0},{0,1},{1,2},{2,3},{3,4},{4,5},{5,6},{6,7},{7,8},{8,9},{9,10... | collective-permute-start | bytes 786440 | tf_op jit(solution)/shard_map/ppermute | solution.py:14
  107.8 19.6 %collective-permute-start.22 = (bf16[128,1024]{1,0:T(8,128)(2,1)}, bf16[128,1024]{1,0:T(8,128)(2,1)}, u32[]{:S(2)}, u32[]{:S(2)}) collective-permute-start(bf16[128,1024]{1,0:T(8,128)(2,1)} %collective-permute-done.18), channel_id=1, source_target_pairs={{1,0},{2,1},{3,2},{4,3},{5,4},{6,5},{7,6},{8,7},{9,8},{10,9},{11,1... | collective-permute-start | bytes 786440 | tf_op jit(solution)/shard_map/ppermute | solution.py:14
  110.1 38.1 %collective-permute-start.23 = (bf16[128,1024]{1,0:T(8,128)(2,1)}, bf16[128,1024]{1,0:T(8,128)(2,1)}, u32[]{:S(2)}, u32[]{:S(2)}) collective-permute-start(bf16[128,1024]{1,0:T(8,128)(2,1)} %collective-permute-done.19), channel_id=1, source_target_pairs={{1,0},{2,1},{3,2},{4,3},{5,4},{6,5},{7,6},{8,7},{9,8},{10,9},{11,1... | collective-permute-start | bytes 786440 | tf_op jit(solution)/shard_map/ppermute | solution.py:14
  116.3 34.2 %collective-permute-start.21 = (bf16[128,1024]{1,0:T(8,128)(2,1)}, bf16[128,1024]{1,0:T(8,128)(2,1)}, u32[]{:S(2)}, u32[]{:S(2)}) collective-permute-start(bf16[128,1024]{1,0:T(8,128)(2,1)} %collective-permute-done.17), channel_id=1, source_target_pairs={{15,0},{0,1},{1,2},{2,3},{3,4},{4,5},{5,6},{6,7},{7,8},{8,9},{9,10... | collective-permute-start | bytes 786440 | tf_op jit(solution)/shard_map/ppermute | solution.py:14
  130.7 10.0 %copy-start.1 = (f32[128,16,128]{0,2,1:T(8,128)S(1)}, f32[128,16,128]{0,2,1:T(8,128)}, u32[]{:S(2)}) copy-start(f32[128,16,128]{0,2,1:T(8,128)} %get-tuple-element.68) | copy-start | bytes 3145732
  130.7 10.0 %copy-start.22 = (bf16[128,1024]{0,1:T(8,128)(2,1)S(1)}, bf16[128,1024]{0,1:T(8,128)(2,1)}, u32[]{:S(2)}) copy-start(bf16[128,1024]{0,1:T(8,128)(2,1)} %copy.70) | copy-start | bytes 786436
  131.9 9.1 %copy-start.20 = (bf16[128,1024]{0,1:T(8,128)(2,1)S(1)}, bf16[128,1024]{0,1:T(8,128)(2,1)}, u32[]{:S(2)}) copy-start(bf16[128,1024]{0,1:T(8,128)(2,1)} %copy.62) | copy-start | bytes 786436
  132.2 9.1 %copy-start.2 = (f32[128,16,128]{0,2,1:T(8,128)S(1)}, f32[128,16,128]{0,2,1:T(8,128)}, u32[]{:S(2)}) copy-start(f32[128,16,128]{0,2,1:T(8,128)} %get-tuple-element.64) | copy-start | bytes 3145732
  132.2 9.1 %copy-start.24 = (bf16[128,1024]{0,1:T(8,128)(2,1)S(1)}, bf16[128,1024]{0,1:T(8,128)(2,1)}, u32[]{:S(2)}) copy-start(bf16[128,1024]{0,1:T(8,128)(2,1)} %copy.76) | copy-start | bytes 786436
  (41 other events, 98.6 us)
where the time goes:
time: 157 us; the launch traced here: 155 us
  local copies, waits for them, and re-layouts  51 us (32%)
  matrix products  40.8 us (26%)
  starting transfers between devices  34.4 us (22%)
  other arithmetic  27.5 us (18%)
    ppermute x24, local copies, waits for them, and re-layouts, from_behind(): return lax.ppermute(block, axis, route)  41.7 us
    ppermute x24, starting transfers between devices, from_behind(): return lax.ppermute(block, axis, route)  34.4 us
    dot_general x13, matrix products, attend_block(): jnp.einsum('qhd,khd->qhk', query3, key3, preferred_element_type=jnp.float32)  27.2 us
    reduce_sum x7, other arithmetic, attend_block(): total = jnp.sum(weights, axis=-1)  9.91 us
    add x1, other arithmetic, combine(): total = total * keep_old + other_total * keep_new  8.35 us
    dot_general x13, matrix products, attend_block(): jnp.einsum('qhk,khd->qhd', weights.astype(jnp.bfloat16), value3, preferre...  7.03 us
    max x1, other arithmetic, combine(): newest = jnp.maximum(peak, other_peak)  6.86 us
    unnamed x98, local copies, waits for them, and re-layouts  4.86 us
  transfers between devices with their start and end apart: 24, of which 0 were waited for; matrix products, arithmetic and copies ran while one was open for 69% of the time, Pallas kernels for 0%

commit v1 on v0

v1 whole, which is shorter than its diff:
```python
import functools

import jax
import jax.numpy as jnp
from jax import lax
from jax.experimental import pallas as pl
from jax.experimental.pallas import tpu as pltpu
from jax.sharding import PartitionSpec as P

HEADS = 16
HEAD_DIM = 64
REACH = 6
SPAN = REACH // 2
SLOTS = 2 * SPAN + 1
MESH = pl.DeviceIdType.MESH
INF = float("inf")

GRID_ROUTE = {1: (0, "down"), 2: (0, "up"), 3: (0, "side"), 4: (1, "side"), 5: (3, "up"), 6: (4, "down")}
GRID_EVENTS = {0: (1, 3, 2), 2: (5, 4), 4: (6,)}


def ring_route():
    route = {1: (0, "down"), 2: (0, "up")}
    for slot in range(3, SLOTS):
        route[slot] = (slot - 2, "down" if slot % 2 else "up")
    events = {2 * i: (2 * i + 1, 2 * i + 2) for i in range(SPAN)}
    return route, events


def is_grid(chips):
    return SPAN == 3 and chips == 2 * SPAN + 2


def neighbour(chip, sign, way, chips):
    if is_grid(chips):
        row, col = chip // 2, chip % 2
        rows = chips // 2
        if way == "side":
            return row * 2 + 1 - col
        step = sign if way == "up" else -sign
        return (row + step + rows) % rows * 2 + col
    step = sign if way == "up" else -sign
    return (chip + step + chips) % chips


def slot_chip(chip, sign, slot, chips):
    if is_grid(chips):
        row, col = chip // 2, chip % 2
        rows = chips // 2
        step, flip = {0: (0, 0), 1: (1, 0), 2: (-1, 0), 3: (0, 1), 4: (1, 1), 5: (-1, 1), 6: (2, 1)}[slot]
        new_col = 1 - col if flip else col
        return (row + step * sign + 2 * rows) % rows * 2 + new_col
    dist = (slot + 1) // 2
    step = dist if slot % 2 else -dist
    return (chip + step * sign + 2 * chips) % chips


def body(
    views, tok_hbm, in_gain, wq_hbm, wk_hbm, wv_hbm, wo_hbm, out_gain, flags,
    out_ref,
    buf, wq, wk, wv, wo, qpad, kbuf, vtbuf, peak, total, acc, peer_flags, mask, hn, hn_in,
    load_sem, send_sem, recv_sem, pass_send, pass_recv, misc_send, misc_recv,
):
    chips = views // 2
    me = lax.axis_index("views")
    chip, core = me // 2, me % 2
    sign = 1 - 2 * core
    partner = chip * 2 + 1 - core
    half = wq.shape[1]
    rows = tok_hbm.shape[0]
    heads = half // HEAD_DIM
    if is_grid(chips):
        route, events = GRID_ROUTE, GRID_EVENTS
        ways = ("up", "down", "side")
    else:
        route, events = ring_route()
        ways = ("up", "down")

    def device(way):
        return {"views": neighbour(chip, sign, way, chips) * 2 + core}

    columns = pl.ds(pl.multiple_of(core * half, half), half)
    loads = [
        pltpu.make_async_copy(tok_hbm, buf.at[0, 0], load_sem.at[0]),
        pltpu.make_async_copy(wq_hbm.at[:, columns], wq, load_sem.at[1]),
        pltpu.make_async_copy(wk_hbm.at[:, columns], wk, load_sem.at[2]),
        pltpu.make_async_copy(wv_hbm.at[:, columns], wv, load_sem.at[3]),
        pltpu.make_async_copy(wo_hbm, wo, load_sem.at[4]),
    ]

    barrier = pltpu.get_barrier_semaphore()
    for way in ways:
        pl.semaphore_signal(barrier, inc=1, device_id=device(way), device_id_type=MESH)
    pl.semaphore_signal(barrier, inc=1, device_id={"views": partner}, device_id_type=MESH)
    for load in loads:
        load.start()
    pl.semaphore_wait(barrier, len(ways) + 1)

    def hop(slot):
        source, way = route[slot]
        return pltpu.make_async_remote_copy(
            src_ref=tok_hbm if source == 0 else buf.at[source, 0],
            dst_ref=buf.at[slot, 0],
            send_sem=send_sem.at[slot],
            recv_sem=recv_sem.at[slot],
            device_id=device(way),
            device_id_type=MESH,
        )

    def hand_over(slot):
        return pltpu.make_async_remote_copy(
            src_ref=tok_hbm if isinstance(slot, int) and slot == 0 else buf.at[slot, 0],
            dst_ref=buf.at[slot, 1],
            send_sem=pass_send.at[slot],
            recv_sem=pass_recv.at[slot],
            device_id={"views": partner},
            device_id_type=MESH,
        )

    flag_copy = pltpu.make_async_remote_copy(
        src_ref=flags, dst_ref=peer_flags, send_sem=misc_send.at[0], recv_sem=misc_recv.at[0],
        device_id={"views": partner}, device_id_type=MESH,
    )
    swap = pltpu.make_async_remote_copy(
        src_ref=hn.at[1], dst_ref=hn_in, send_sem=misc_send.at[1], recv_sem=misc_recv.at[1],
        device_id={"views": partner}, device_id_type=MESH,
    )
    hand_over(0).start()
    flag_copy.start()
    for slot in route:
        if route[slot][0] == 0:
            hop(slot).start()

    peak[...] = jnp.full(peak.shape, -INF, jnp.float32)
    total[...] = jnp.zeros(total.shape, jnp.float32)
    acc[...] = jnp.zeros(acc.shape, jnp.float32)
    flag_copy.wait_recv()
    for slot in range(SLOTS):
        for bank in range(2):
            own_row = flags[pl.ds(2 * slot + bank, 1), :]
            peer_row = peer_flags[pl.ds(2 * slot + 1 - bank, 1), :]
            mask[slot, pl.ds(bank, 1), :] = jnp.concatenate([own_row, peer_row], axis=1)

    def normed_of(slot):
        raw = buf[slot].reshape(2 * rows, buf.shape[-1]).astype(jnp.float32)
        mean_sq = jnp.mean(raw * raw, axis=-1, keepdims=True)
        return (raw * lax.rsqrt(mean_sq + 1e-6) * in_gain[...]).astype(jnp.bfloat16)

    loads[0].wait()
    hand_over(0).wait_recv()
    loads[1].wait()
    query = jnp.dot(normed_of(0), wq[...], preferred_element_type=jnp.float32).astype(jnp.bfloat16)
    query = query.astype(jnp.float32) * HEAD_DIM ** (-0.5)
    query_t = query.T.astype(jnp.bfloat16)
    zero = jnp.zeros((HEAD_DIM, 2 * rows), jnp.bfloat16)
    for h in range(heads):
        mine = query_t[h * HEAD_DIM:(h + 1) * HEAD_DIM, :]
        qpad[h] = jnp.concatenate([mine, zero] if h % 2 == 0 else [zero, mine], axis=0)
    loads[2].wait()
    loads[3].wait()

    def chunk(slot, carry):
        @pl.when(slot > 0)
        def _():
            hand_over(slot).wait_recv()

        normed = normed_of(slot)
        kbuf[...] = jnp.dot(normed, wk[...], preferred_element_type=jnp.float32).astype(jnp.bfloat16)
        value = jnp.dot(normed, wv[...], preferred_element_type=jnp.float32)
        vtbuf[...] = value.T.astype(jnp.bfloat16)
        live = mask[slot]
        on_first = live[0:1, :] > 0.5
        on_second = live[1:2, :] > 0.5
        for h in range(heads):
            pair = (h // 2) * 2 * HEAD_DIM
            feats = slice(h * HEAD_DIM, (h + 1) * HEAD_DIM)
            scores = jnp.dot(
                kbuf[:, pair:pair + 2 * HEAD_DIM], qpad[h], preferred_element_type=jnp.float32
            )
            first, second = scores[:rows], scores[rows:]
            old = peak[h:h + 1, :]
            new = jnp.maximum(
                jnp.where(on_first, jnp.max(first, axis=0, keepdims=True), -INF),
                jnp.where(on_second, jnp.max(second, axis=0, keepdims=True), -INF),
            )
            new = jnp.maximum(old, new)
            e_first = jnp.exp(first - jnp.where(on_first, new, INF))
            e_second = jnp.exp(second - jnp.where(on_second, new, INF))
            keep = jnp.exp(old - new)
            peak[h:h + 1, :] = new
            total[h:h + 1, :] = total[h:h + 1, :] * keep + jnp.sum(e_first + e_second, axis=0, keepdims=True)
            weights = jnp.concatenate([e_first, e_second], axis=0).astype(jnp.bfloat16)
            acc[feats, :] = acc[feats, :] * keep + jnp.dot(
                vtbuf[feats, :], weights, preferred_element_type=jnp.float32
            )

        for after, arrivals in events.items():
            @pl.when(slot == after)
            def _(arrivals=arrivals):
                for got in arrivals:
                    hop(got).wait_recv()
                    hand_over(got).start()
                    for later in route:
                        if route[later][0] == got:
                            hop(later).start()
        return carry

    lax.fori_loop(0, SLOTS, chunk, 0)

    gain = out_gain[:, columns]
    pieces = []
    for h in range(heads):
        attended = acc[h * HEAD_DIM:(h + 1) * HEAD_DIM, :] / total[h:h + 1, :]
        mean_sq = jnp.mean(attended * attended, axis=0, keepdims=True)
        pieces.append(attended * lax.rsqrt(mean_sq + 1e-6))
    head_normed = (jnp.concatenate(pieces, axis=0).T * gain).astype(jnp.bfloat16)
    hn[1] = head_normed[rows:]
    swap.start()
    hn[0] = head_normed[:rows]
    loads[4].wait()
    others = pl.ds(pl.multiple_of((1 - core) * half, half), half)
    update = jnp.dot(hn[0], wo[columns, :], preferred_element_type=jnp.float32)
    swap.wait_recv()
    update = update + jnp.dot(hn_in[...], wo[others, :], preferred_element_type=jnp.float32)
    out_ref[...] = (buf[0, 0].astype(jnp.float32) + update).astype(out_ref.dtype)

    for slot in route:
        hop(slot).wait_send()
    for slot in range(SLOTS):
        hand_over(slot).wait_send()
    flag_copy.wait_send()
    swap.wait_send()


def on_device(tokens, in_gain, w_query, w_key, w_value, w_out, out_gain, covis_list, covis_count):
    views = lax.axis_size("views")
    chips = views // 2
    me = lax.axis_index("views")
    chip, core = me // 2, me % 2
    sign = 1 - 2 * core
    rows, width = tokens.shape[1:]
    half = width // 2
    ids = []
    for slot in range(SLOTS):
        ids.append(slot_chip(chip, sign, slot, chips) * 2 + core)
        ids.append(slot_chip(chip, -sign, slot, chips) * 2 + 1 - core)
    ids += [-1] * (16 - len(ids))
    ids = jnp.stack([jnp.asarray(i, jnp.int32) for i in ids])
    valid = jnp.arange(covis_list.shape[1], dtype=jnp.int32) < covis_count[0]
    listed = jnp.any((covis_list[0][None, :] == ids[:, None]) & valid[None, :], axis=1) | (ids == me)
    flags = jnp.broadcast_to(listed.astype(jnp.float32)[:, None], (16, rows))
    hbm = pl.BlockSpec(memory_space=pl.ANY)
    vmem = pl.BlockSpec(memory_space=pltpu.VMEM)
    bf16, f32 = jnp.bfloat16, jnp.float32
    heads = half // HEAD_DIM
    dma = pltpu.SemaphoreType.DMA
    out = pl.pallas_call(
        functools.partial(body, views),
        out_shape=jax.ShapeDtypeStruct((rows, width), tokens.dtype),
        in_specs=[hbm, vmem, hbm, hbm, hbm, hbm, vmem, vmem],
        out_specs=vmem,
        scratch_shapes=[
            pltpu.VMEM((SLOTS, 2, rows, width), bf16),
            pltpu.VMEM((width, half), bf16),
            pltpu.VMEM((width, half), bf16),
            pltpu.VMEM((width, half), bf16),
            pltpu.VMEM((width, width), bf16),
            pltpu.VMEM((heads, 2 * HEAD_DIM, 2 * rows), bf16),
            pltpu.VMEM((2 * rows, half), bf16),
            pltpu.VMEM((half, 2 * rows), bf16),
            pltpu.VMEM((heads, 2 * rows), f32),
            pltpu.VMEM((heads, 2 * rows), f32),
            pltpu.VMEM((half, 2 * rows), f32),
            pltpu.VMEM((16, rows), f32),
            pltpu.VMEM((SLOTS, 2, 2 * rows), f32),
            pltpu.VMEM((2, rows, half), bf16),
            pltpu.VMEM((rows, half), bf16),
            dma((5,)),
            dma((SLOTS,)),
            dma((SLOTS,)),
            dma((SLOTS,)),
            dma((SLOTS,)),
            dma((2,)),
            dma((2,)),
        ],
        compiler_params=pltpu.CompilerParams(
            collective_id=0, has_side_effects=True, vmem_limit_bytes=48 * 1024 * 1024
        ),
    )(tokens[0], in_gain[None], w_query, w_key, w_value, w_out, out_gain[None], flags)
    return out[None]


def solution(mesh):
    in_specs = (
        P(("groups", "views"), None, None),
        P(), P(), P(), P(), P(), P(),
        P(("groups", "views"), None),
        P(("groups", "views")),
    )
    out_specs = P(("groups", "views"), None, None)
    return jax.shard_map(on_device, mesh=mesh, in_specs=in_specs, out_specs=out_specs, check_vma=False)
```

time: 157 us -> 48.6 us (0.31)
  local copies, waits for them, and re-layouts: 51 us -> 6.39 us
  matrix products: 40.8 us -> 0 us
  Pallas kernels: 0 us -> 40.3 us
  starting transfers between devices: 34.4 us -> 0 us
  other arithmetic: 27.5 us -> 0.86 us
    ppermute x24 -> x0, local copies, waits for them, and re-layouts: 41.7 us -> none  [from_behind(): return lax.ppermute(block, axis, route)]
    dot_general x30 -> x0, matrix products: 40.8 us -> none  [the longest x13 27.2 us: attend_block(): jnp.einsum('qhd,khd->qhk', query3, key3, preferred_element_type=jnp.float32)]
    pallas_call x0 -> x1, Pallas kernels: none -> 40.3 us  [on_device(): pl.pallas_call(functools.partial(body, views), out_shape=jax.ShapeDtypeSt...]
    ppermute x24 -> x0, starting transfers between devices: 34.4 us -> none  [from_behind(): return lax.ppermute(block, axis, route)]
    reduce_sum x8 -> x0, other arithmetic: 11.1 us -> none  [the longest x7 9.91 us: attend_block(): total = jnp.sum(weights, axis=-1)]
    add x1 -> x0, other arithmetic: 8.35 us -> none  [combine(): total = total * keep_old + other_total * keep_new]
    max x1 -> x0, other arithmetic: 6.86 us -> none  [combine(): newest = jnp.maximum(peak, other_peak)]
    convert_element_type x3 -> x0, local copies, waits for them, and re-layouts: 3.8 us -> none  [the longest x1 1.83 us: on_device(): jnp.dot(normed, w_key, preferred_element_type=jnp.float32)]
  transfers between devices with their start and end apart: 24 -> 0, of which waited for: 0 -> 0; matrix products, arithmetic and copies ran while one was open for 69% -> 0% of each run, Pallas kernels for 0% -> 0%
where the time goes in v1:
time: 48.6 us; the launch traced here: 48.3 us
  Pallas kernels  40.3 us (83%)
  local copies, waits for them, and re-layouts  6.39 us (13%)
  other arithmetic  0.86 us (2%)
  between operations  0.69 us (1%)
    pallas_call x1, Pallas kernels, on_device(): pl.pallas_call(functools.partial(body, views), out_shape=jax.ShapeDtypeSt...  40.3 us
    unnamed x11, local copies, waits for them, and re-layouts  6.21 us

profile of v1, /device:TPU:1, one launch (start us, length us, event | category | flops | bytes accessed | tf_op | source)
XLA Modules:
  0.0 48.3 jit_solution(9665420130796852039)
XLA Ops:
  0.7 0.1 stack.59
  0.8 0.8 %and_reduce_fusion = pred[16]{0:T(512)(128)(4,1)S(1)} fusion(s32[12]{0:T(128)} %bitcast.25, s32[16]{0:T(128)S(1)} %stack.59, pred[12]{0:T(512)(128)(4,1)S(1)} %iota_compare_fusion), kind=kLoop, calls=%fused_computation | loop fusion | flops 560 | bytes 140 | tf_op jit(solution)/shard_map/reduce_or | solution.py:250
  1.6 0.1 broadcast_in_dim.19.flags
  1.7 0.0 copy-start
  1.7 1.6 %copy-done = bf16[1024,1024]{1,0:T(8,128)(2,1)S(1)} copy-done((bf16[1024,1024]{1,0:T(8,128)(2,1)S(1)}, bf16[1024,1024]{1,0:T(8,128)(2,1)}, u32[]{:S(2)}) %copy-start) | copy-done | bytes 2097176
  3.3 0.0 copy-start.1
  3.3 1.6 %copy-done.1 = bf16[1024,1024]{1,0:T(8,128)(2,1)S(1)} copy-done((bf16[1024,1024]{1,0:T(8,128)(2,1)S(1)}, bf16[1024,1024]{1,0:T(8,128)(2,1)}, u32[]{:S(2)}) %copy-start.1) | copy-done | bytes 2097176
  4.9 0.0 copy-start.2
  4.9 0.9 %copy-done.2 = bf16[1,128,1024]{2,1,0:T(8,128)(2,1)S(1)} copy-done((bf16[1,128,1024]{2,1,0:T(8,128)(2,1)S(1)}, bf16[1,128,1024]{2,1,0:T(8,128)(2,1)}, u32[]{:S(2)}) %copy-start.2) | copy-done | bytes 262168
  5.8 0.0 copy-start.3
  5.8 0.7 %copy-done.3 = f32[1024]{0:T(1024)S(1)} copy-done((f32[1024]{0:T(1024)S(1)}, f32[1024]{0:T(1024)}, u32[]{:S(2)}) %copy-start.3) | copy-done | bytes 4120
  6.5 0.0 copy-start.4
  6.5 0.7 %copy-done.4 = f32[1024]{0:T(1024)S(1)} copy-done((f32[1024]{0:T(1024)S(1)}, f32[1024]{0:T(1024)}, u32[]{:S(2)}) %copy-start.4) | copy-done | bytes 4120
  7.2 40.3 %shard_map.91 = bf16[128,1024]{1,0:T(8,128)(2,1)S(1)} custom-call(bf16[128,1024]{1,0:T(8,128)(2,1)S(1)} %bitcast.22, f32[1,1024]{1,0:T(1,128)S(1)} %bitcast.23, bf16[1024,1024]{1,0:T(8,128)(2,1)S(1)} %copy-done, bf16[1024,1024]{1,0:T(8,128)(2,1)S(1)} %copy-done.1, bf16[1024,1024]{1,0:T(8,128)(2,1)} %wv_hbm.1, bf16[1024,1024]{1,0:T(8,128)(2,1)} %wo_hbm.1, ...), custom_call_target="tpu_custom_call" | custom-call | tf_op jit(solution)/shard_map/pallas_call | solution.py:257
  47.6 0.7 %copy.12 = bf16[1,128,1024]{2,1,0:T(8,128)(2,1)} copy(bf16[1,128,1024]{2,1,0:T(8,128)(2,1)S(1)} %bitcast.21) | data formatting | bytes 524288
  (3 shorter events, 0.0 us)
Async XLA Ops:
  1.7 1.6 %copy-start = (bf16[1024,1024]{1,0:T(8,128)(2,1)S(1)}, bf16[1024,1024]{1,0:T(8,128)(2,1)}, u32[]{:S(2)}) copy-start(bf16[1024,1024]{1,0:T(8,128)(2,1)} %wq_hbm.1) | copy-start | bytes 6291460
  3.3 1.6 %copy-start.1 = (bf16[1024,1024]{1,0:T(8,128)(2,1)S(1)}, bf16[1024,1024]{1,0:T(8,128)(2,1)}, u32[]{:S(2)}) copy-start(bf16[1024,1024]{1,0:T(8,128)(2,1)} %wk_hbm.1) | copy-start | bytes 6291460
  4.9 0.9 %copy-start.2 = (bf16[1,128,1024]{2,1,0:T(8,128)(2,1)S(1)}, bf16[1,128,1024]{2,1,0:T(8,128)(2,1)}, u32[]{:S(2)}) copy-start(bf16[1,128,1024]{2,1,0:T(8,128)(2,1)} %param.9) | copy-start | bytes 786436
  5.8 0.7 %copy-start.3 = (f32[1024]{0:T(1024)S(1)}, f32[1024]{0:T(1024)}, u32[]{:S(2)}) copy-start(f32[1024]{0:T(1024)} %param.10) | copy-start | bytes 12292
  6.5 0.7 %copy-start.4 = (f32[1024]{0:T(1024)S(1)}, f32[1024]{0:T(1024)}, u32[]{:S(2)}) copy-start(f32[1024]{0:T(1024)} %param.15) | copy-start | bytes 12292

commit v2 on v1

--- a/solution.py
+++ b/solution.py
@@ -56,9 +56,9 @@
 
 
 def body(
-    views, tok_hbm, in_gain, wq_hbm, wk_hbm, wv_hbm, wo_hbm, out_gain, flags,
+    views, tok_hbm, in_gain_hbm, wq_hbm, wk_hbm, wv_hbm, wo_hbm, out_gain_hbm, list_hbm, count_hbm,
     out_ref,
-    buf, wq, wk, wv, wo, qpad, kbuf, vtbuf, peak, total, acc, peer_flags, mask, hn, hn_in,
+    buf, wq, wk, wv, wo, in_gain, out_gain, lists, counts, qpad, kbuf, vtbuf, peak, total, acc, mask, hn, hn_in,
     load_sem, send_sem, recv_sem, pass_send, pass_recv, misc_send, misc_recv,
 ):
     chips = views // 2
@@ -86,6 +86,10 @@
         pltpu.make_async_copy(wk_hbm.at[:, columns], wk, load_sem.at[2]),
         pltpu.make_async_copy(wv_hbm.at[:, columns], wv, load_sem.at[3]),
         pltpu.make_async_copy(wo_hbm, wo, load_sem.at[4]),
+        pltpu.make_async_copy(in_gain_hbm, in_gain, load_sem.at[5]),
+        pltpu.make_async_copy(out_gain_hbm, out_gain, load_sem.at[6]),
+        pltpu.make_async_copy(list_hbm, lists.at[0], load_sem.at[7]),
+        pltpu.make_async_copy(count_hbm, counts.at[0], load_sem.at[8]),
     ]
 
     barrier = pltpu.get_barrier_semaphore()
@@ -117,8 +121,12 @@
             device_id_type=MESH,
         )
 
-    flag_copy = pltpu.make_async_remote_copy(
-        src_ref=flags, dst_ref=peer_flags, send_sem=misc_send.at[0], recv_sem=misc_recv.at[0],
+    list_copy = pltpu.make_async_remote_copy(
+        src_ref=list_hbm, dst_ref=lists.at[1], send_sem=misc_send.at[0], recv_sem=misc_recv.at[0],
+        device_id={"views": partner}, device_id_type=MESH,
+    )
+    count_copy = pltpu.make_async_remote_copy(
+        src_ref=count_hbm, dst_ref=counts.at[1], send_sem=misc_send.at[2], recv_sem=misc_recv.at[2],
         device_id={"views": partner}, device_id_type=MESH,
     )
     swap = pltpu.make_async_remote_copy(
@@ -126,7 +134,8 @@
         device_id={"views": partner}, device_id_type=MESH,
     )
     hand_over(0).start()
-    flag_copy.start()
+    list_copy.start()
+    count_copy.start()
     for slot in route:
         if route[slot][0] == 0:
             hop(slot).start()
@@ -134,12 +143,23 @@
     peak[...] = jnp.full(peak.shape, -INF, jnp.float32)
     total[...] = jnp.zeros(total.shape, jnp.float32)
     acc[...] = jnp.zeros(acc.shape, jnp.float32)
-    flag_copy.wait_recv()
+    for load in loads[5:]:
+        load.wait()
+    list_copy.wait_recv()
+    count_copy.wait_recv()
+    ids = jnp.zeros((16, 1), jnp.int32)
+    place = lax.broadcasted_iota(jnp.int32, (16, 1), 0)
     for slot in range(SLOTS):
-        for bank in range(2):
-            own_row = flags[pl.ds(2 * slot + bank, 1), :]
-            peer_row = peer_flags[pl.ds(2 * slot + 1 - bank, 1), :]
-            mask[slot, pl.ds(bank, 1), :] = jnp.concatenate([own_row, peer_row], axis=1)
+        mine = slot_chip(chip, sign, slot, chips) * 2 + core
+        other = slot_chip(chip, -sign, slot, chips) * 2 + 1 - core
+        ids = jnp.where(place == 2 * slot, mine, jnp.where(place == 2 * slot + 1, other, ids))
+    for side, query_view in enumerate((me, partner)):
+        listed = lists[side]
+        valid = lax.broadcasted_iota(jnp.int32, (16, listed.shape[1]), 1) < counts[side:side + 1, :]
+        hits = jnp.where(((listed == ids) | (ids == query_view)) & valid, 1.0, 0.0)
+        mask[:, side * rows:(side + 1) * rows] = jnp.broadcast_to(
+            jnp.max(hits, axis=1, keepdims=True), (16, rows)
+        )
 
     def normed_of(slot):
         raw = buf[slot].reshape(2 * rows, buf.shape[-1]).astype(jnp.float32)
@@ -168,9 +188,8 @@
         kbuf[...] = jnp.dot(normed, wk[...], preferred_element_type=jnp.float32).astype(jnp.bfloat16)
         value = jnp.dot(normed, wv[...], preferred_element_type=jnp.float32)
         vtbuf[...] = value.T.astype(jnp.bfloat16)
-        live = mask[slot]
-        on_first = live[0:1, :] > 0.5
-        on_second = live[1:2, :] > 0.5
+        on_first = mask[pl.ds(2 * slot, 1), :] > 0.5
+        on_second = mask[pl.ds(2 * slot + 1, 1), :] > 0.5
         for h in range(heads):
             pair = (h // 2) * 2 * HEAD_DIM
             feats = slice(h * HEAD_DIM, (h + 1) * HEAD_DIM)
@@ -228,28 +247,17 @@
         hop(slot).wait_send()
     for slot in range(SLOTS):
         hand_over(slot).wait_send()
-    flag_copy.wait_send()
+    list_copy.wait_send()
+    count_copy.wait_send()
     swap.wait_send()
 
 
 def on_device(tokens, in_gain, w_query, w_key, w_value, w_out, out_gain, covis_list, covis_count):
     views = lax.axis_size("views")
-    chips = views // 2
-    me = lax.axis_index("views")
-    chip, core = me // 2, me % 2
-    sign = 1 - 2 * core
     rows, width = tokens.shape[1:]
     half = width // 2
-    ids = []
-    for slot in range(SLOTS):
-        ids.append(slot_chip(chip, sign, slot, chips) * 2 + core)
-        ids.append(slot_chip(chip, -sign, slot, chips) * 2 + 1 - core)
-    ids += [-1] * (16 - len(ids))
-    ids = jnp.stack([jnp.asarray(i, jnp.int32) for i in ids])
-    valid = jnp.arange(covis_list.shape[1], dtype=jnp.int32) < covis_count[0]
-    listed = jnp.any((covis_list[0][None, :] == ids[:, None]) & valid[None, :], axis=1) | (ids == me)
-    flags = jnp.broadcast_to(listed.astype(jnp.float32)[:, None], (16, rows))
-    hbm = pl.BlockSpec(memory_space=pl.ANY)
+    slots_listed = covis_list.shape[1]
+    hbm = pl.BlockSpec(memory_space=pltpu.HBM)
     vmem = pl.BlockSpec(memory_space=pltpu.VMEM)
     bf16, f32 = jnp.bfloat16, jnp.float32
     heads = half // HEAD_DIM
@@ -257,7 +265,7 @@
     out = pl.pallas_call(
         functools.partial(body, views),
         out_shape=jax.ShapeDtypeStruct((rows, width), tokens.dtype),
-        in_specs=[hbm, vmem, hbm, hbm, hbm, hbm, vmem, vmem],
+        in_specs=[hbm] * 9,
         out_specs=vmem,
         scratch_shapes=[
             pltpu.VMEM((SLOTS, 2, rows, width), bf16),
@@ -265,28 +273,31 @@
             pltpu.VMEM((width, half), bf16),
             pltpu.VMEM((width, half), bf16),
             pltpu.VMEM((width, width), bf16),
+            pltpu.VMEM((1, width), f32),
+            pltpu.VMEM((1, width), f32),
+            pltpu.VMEM((2, 1, slots_listed), jnp.int32),
+            pltpu.VMEM((2, 1), jnp.int32),
             pltpu.VMEM((heads, 2 * HEAD_DIM, 2 * rows), bf16),
             pltpu.VMEM((2 * rows, half), bf16),
             pltpu.VMEM((half, 2 * rows), bf16),
             pltpu.VMEM((heads, 2 * rows), f32),
             pltpu.VMEM((heads, 2 * rows), f32),
             pltpu.VMEM((half, 2 * rows), f32),
-            pltpu.VMEM((16, rows), f32),
-            pltpu.VMEM((SLOTS, 2, 2 * rows), f32),
+            pltpu.VMEM((16, 2 * rows), f32),
             pltpu.VMEM((2, rows, half), bf16),
             pltpu.VMEM((rows, half), bf16),
-            dma((5,)),
+            dma((9,)),
             dma((SLOTS,)),
             dma((SLOTS,)),
             dma((SLOTS,)),
             dma((SLOTS,)),
-            dma((2,)),
-            dma((2,)),
+            dma((3,)),
+            dma((3,)),
         ],
         compiler_params=pltpu.CompilerParams(
-            collective_id=0, has_side_effects=True, vmem_limit_bytes=48 * 1024 * 1024
+            collective_id=0, has_side_effects=True, vmem_limit_bytes=60 * 1024 * 1024
         ),
-    )(tokens[0], in_gain[None], w_query, w_key, w_value, w_out, out_gain[None], flags)
+    )(tokens[0], in_gain[None], w_query, w_key, w_value, w_out, out_gain[None], covis_list, covis_count)
     return out[None]
 
 

time: 48.6 us -> 43.7 us (0.90)
  local copies, waits for them, and re-layouts: 6.39 us -> 1.67 us
  Pallas kernels: 40.3 us -> 41.2 us
  other arithmetic: 0.86 us -> 0 us
    unnamed x11 -> x1, local copies, waits for them, and re-layouts: 6.21 us -> 1.67 us
    pallas_call x1, Pallas kernels: 40.3 us -> 41.2 us  [on_device(): pl.pallas_call(functools.partial(body, views), out_shape=jax.ShapeDtypeSt...]
    reduce_or x1 -> x0, other arithmetic: 0.84 us -> none  [on_device(): jnp.any((covis_list[0][None, :] == ids[:, None]) & valid[None, :], axis=1)]
where the time goes in v2:
time: 43.7 us; the launch traced here: 43.6 us
  Pallas kernels  41.2 us (94%)
  local copies, waits for them, and re-layouts  1.67 us (4%)
  between operations  0.66 us (2%)
    pallas_call x1, Pallas kernels, on_device(): pl.pallas_call(functools.partial(body, views), out_shape=jax.ShapeDtypeSt...  41.2 us
    unnamed x1, local copies, waits for them, and re-layouts  1.67 us

profile of v2, /device:TPU:1, one launch (start us, length us, event | category | flops | bytes accessed | tf_op | source)
XLA Modules:
  0.0 43.6 jit_solution(14050635562839261310)
XLA Ops:
  0.7 41.2 %shard_map.91 = bf16[128,1024]{1,0:T(8,128)(2,1)} custom-call(bf16[128,1024]{1,0:T(8,128)(2,1)} %bitcast.5, f32[1,1024]{1,0:T(1,128)} %bitcast.6, bf16[1024,1024]{1,0:T(8,128)(2,1)} %wq_hbm.1, bf16[1024,1024]{1,0:T(8,128)(2,1)} %wk_hbm.1, bf16[1024,1024]{1,0:T(8,128)(2,1)} %wv_hbm.1, bf16[1024,1024]{1,0:T(8,128)(2,1)} %wo_hbm.1, f32[1,1024]{1,0:T(1,128)} %bitcast.7, ...), custom_call_target="tpu_custom_call" | custom-call | tf_op jit(solution)/shard_map/pallas_call | solution.py:265
  41.9 1.7 %copy.12 = bf16[1,128,1024]{2,1,0:T(8,128)(2,1)} copy(bf16[1,128,1024]{2,1,0:T(8,128)(2,1)} %bitcast.4) | data formatting | bytes 524288

commit v3 on v2

v3 whole, which is shorter than its diff:
```python
import functools

import jax
import jax.numpy as jnp
from jax import lax
from jax.experimental import pallas as pl
from jax.experimental.pallas import tpu as pltpu
from jax.sharding import PartitionSpec as P

HEADS = 16
HEAD_DIM = 64
REACH = 6
SPAN = REACH // 2
CHUNKS = 2 * SPAN + 1
PARTS = 4
MESH = pl.DeviceIdType.MESH
INF = float("inf")


def is_grid(chips):
    return chips == 2 * SPAN + 2


def ring_position(chip, chips):
    if not is_grid(chips):
        return chip
    row, col = chip // 2, chip % 2
    return row + col * (chips - 1 - 2 * row)


def ring_chip(position, chips):
    position = (position + chips) % chips
    if not is_grid(chips):
        return position
    col = position // (chips // 2)
    row = position + col * (chips - 1 - 2 * position)
    return 2 * row + col


def ring_route(chips):
    route = {1: (0, -1), 2: (0, 1)}
    last = CHUNKS + 1 if is_grid(chips) else CHUNKS
    for slot in range(3, last):
        route[slot] = (slot - 2, -1 if slot % 2 else 1)
    arrive, settle = {}, {}
    for first in range(1, last, 2):
        hops = (first + 1) // 2
        pair = [slot for slot in (first, first + 1) if slot in route]
        need = 2 * hops - 1
        if is_grid(chips) and hops >= SPAN:
            need = 2 * hops - 2
        for part in range(PARTS):
            after = need - 1
            if hops == 2 or not is_grid(chips) and hops == SPAN:
                after = need - 2 + part * 2 // PARTS
            if hops > SPAN:
                after = need - 2
            for slot in pair:
                arrive.setdefault(after, []).append((slot, part))
                settle.setdefault(need, []).append((slot, part))
    return route, arrive, settle


def slot_of(chunk, position, sign, chips):
    if not is_grid(chips):
        return chunk
    late = position % (chips // 2) // (chips // 4)
    ahead = (1 - 2 * late) * sign
    skipped = (SPAN + 1) - (ahead + 1) // 2
    return chunk + (chunk >= skipped).astype(jnp.int32)


def body(
    views, tok_hbm, in_gain_hbm, wq_hbm, wk_hbm, wv_hbm, wo_hbm, out_gain_hbm, list_hbm, count_hbm,
    out_ref,
    buf, wq, wk, wv, wo, in_gain, out_gain, lists, counts, qpad, kbuf, vtbuf, peak, total, acc, mask, hn, hn_in,
    load_sem, send_sem, recv_sem, pass_send, pass_recv, misc_send, misc_recv,
):
    chips = views // 2
    me = lax.axis_index("views")
    chip, core = me // 2, me % 2
    sign = 1 - 2 * core
    place = ring_position(chip, chips)
    partner = chip * 2 + 1 - core
    half = wq.shape[1]
    rows = tok_hbm.shape[0]
    heads = half // HEAD_DIM
    route, arrive, settle = ring_route(chips)

    def device(step):
        return {"views": ring_chip(place + step * sign, chips) * 2 + core}

    columns = pl.ds(pl.multiple_of(core * half, half), half)
    loads = [
        pltpu.make_async_copy(tok_hbm, buf.at[0, 0], load_sem.at[0]),
        pltpu.make_async_copy(wq_hbm.at[:, columns], wq, load_sem.at[1]),
        pltpu.make_async_copy(wk_hbm.at[:, columns], wk, load_sem.at[2]),
        pltpu.make_async_copy(wv_hbm.at[:, columns], wv, load_sem.at[3]),
        pltpu.make_async_copy(wo_hbm, wo, load_sem.at[4]),
        pltpu.make_async_copy(in_gain_hbm, in_gain, load_sem.at[5]),
        pltpu.make_async_copy(out_gain_hbm, out_gain, load_sem.at[6]),
        pltpu.make_async_copy(list_hbm, lists.at[0], load_sem.at[7]),
        pltpu.make_async_copy(count_hbm, counts.at[0], load_sem.at[8]),
    ]

    barrier = pltpu.get_barrier_semaphore()
    for way in (-1, 1):
        pl.semaphore_signal(barrier, inc=1, device_id=device(way), device_id_type=MESH)
    pl.semaphore_signal(barrier, inc=1, device_id={"views": partner}, device_id_type=MESH)
    for load in loads:
        load.start()
    pl.semaphore_wait(barrier, 3)

    size = rows // PARTS

    def hop(slot, part):
        source, step = route[slot]
        span = pl.ds(part * size, size)
        return pltpu.make_async_remote_copy(
            src_ref=tok_hbm.at[span] if source == 0 else buf.at[source, 0, span],
            dst_ref=buf.at[slot, 0, span],
            send_sem=send_sem.at[slot, part],
            recv_sem=recv_sem.at[slot, part],
            device_id=device(step),
            device_id_type=MESH,
        )

    def hand_over(slot, part):
        span = pl.ds(part * size, size)
        return pltpu.make_async_remote_copy(
            src_ref=tok_hbm.at[span] if slot == 0 else buf.at[slot, 0, span],
            dst_ref=buf.at[slot, 1, span],
            send_sem=pass_send.at[slot, part],
            recv_sem=pass_recv.at[slot, part],
            device_id={"views": partner},
            device_id_type=MESH,
        )

    list_copy = pltpu.make_async_remote_copy(
        src_ref=list_hbm, dst_ref=lists.at[1], send_sem=misc_send.at[0], recv_sem=misc_recv.at[0],
        device_id={"views": partner}, device_id_type=MESH,
    )
    count_copy = pltpu.make_async_remote_copy(
        src_ref=count_hbm, dst_ref=counts.at[1], send_sem=misc_send.at[2], recv_sem=misc_recv.at[2],
        device_id={"views": partner}, device_id_type=MESH,
    )
    swap = pltpu.make_async_remote_copy(
        src_ref=hn.at[1], dst_ref=hn_in, send_sem=misc_send.at[1], recv_sem=misc_recv.at[1],
        device_id={"views": partner}, device_id_type=MESH,
    )
    parts = range(PARTS)
    list_copy.start()
    count_copy.start()
    for part in parts:
        hand_over(0, part).start()
        for slot in route:
            if route[slot][0] == 0:
                hop(slot, part).start()

    peak[...] = jnp.full(peak.shape, -INF, jnp.float32)
    total[...] = jnp.zeros(total.shape, jnp.float32)
    acc[...] = jnp.zeros(acc.shape, jnp.float32)
    for load in loads[5:]:
        load.wait()
    list_copy.wait_recv()
    count_copy.wait_recv()
    ids = jnp.zeros((16, 1), jnp.int32)
    line = lax.broadcasted_iota(jnp.int32, (16, 1), 0)
    for t in range(CHUNKS):
        for bank in range(2):
            way = sign * (1 - 2 * bank)
            slot = slot_of(jnp.int32(t), place, way, chips)
            odd = slot % 2
            step = (slot + 1) // 2 * (2 * odd - 1) * way
            view = ring_chip(place + step, chips) * 2 + (core if bank == 0 else 1 - core)
            ids = jnp.where(line == 2 * t + bank, view, ids)
    for side, query_view in enumerate((me, partner)):
        listed = lists[side]
        valid = lax.broadcasted_iota(jnp.int32, (16, listed.shape[1]), 1) < counts[side:side + 1, :]
        hits = jnp.where(((listed == ids) | (ids == query_view)) & valid, 1.0, 0.0)
        mask[:, side * rows:(side + 1) * rows] = jnp.broadcast_to(
            jnp.max(hits, axis=1, keepdims=True), (16, rows)
        )

    def normed_of(first, second):
        raw = jnp.concatenate([buf[first, 0], buf[second, 1]], axis=0).astype(jnp.float32)
        mean_sq = jnp.mean(raw * raw, axis=-1, keepdims=True)
        return (raw * lax.rsqrt(mean_sq + 1e-6) * in_gain[...]).astype(jnp.bfloat16)

    loads[0].wait()
    for part in parts:
        hand_over(0, part).wait_recv()
    loads[1].wait()
    query = jnp.dot(normed_of(0, 0), wq[...], preferred_element_type=jnp.float32).astype(jnp.bfloat16)
    query = query.astype(jnp.float32) * HEAD_DIM ** (-0.5)
    query_t = query.T.astype(jnp.bfloat16)
    zero = jnp.zeros((HEAD_DIM, 2 * rows), jnp.bfloat16)
    for h in range(heads):
        mine = query_t[h * HEAD_DIM:(h + 1) * HEAD_DIM, :]
        qpad[h] = jnp.concatenate([mine, zero] if h % 2 == 0 else [zero, mine], axis=0)
    loads[2].wait()
    loads[3].wait()

    def chunk(slot, carry):
        for ahead_of, handed in settle.items():
            @pl.when(slot == ahead_of)
            def _(handed=handed):
                for got, part in handed:
                    hand_over(got, part).wait_recv()

        near = slot_of(slot, place, sign, chips)
        far = slot_of(slot, place, -sign, chips)
        normed = normed_of(near, far)
        kbuf[...] = jnp.dot(normed, wk[...], preferred_element_type=jnp.float32).astype(jnp.bfloat16)
        value = jnp.dot(normed, wv[...], preferred_element_type=jnp.float32)
        vtbuf[...] = value.T.astype(jnp.bfloat16)
        on_first = mask[pl.ds(2 * slot, 1), :] > 0.5
        on_second = mask[pl.ds(2 * slot + 1, 1), :] > 0.5
        def scores_of(h):
            pair = (h // 2) * 2 * HEAD_DIM
            return jnp.dot(kbuf[:, pair:pair + 2 * HEAD_DIM], qpad[h], preferred_element_type=jnp.float32)

        waiting = scores_of(0)
        pend = None
        def finish(p):
            h, keep, weights = p
            feats = slice(h * HEAD_DIM, (h + 1) * HEAD_DIM)
            acc[feats, :] = acc[feats, :] * keep + jnp.dot(vtbuf[feats, :], weights, preferred_element_type=jnp.float32)
        peaks, totals = peak[...], total[...]
        new_peaks, new_totals = [], []
        for h in range(heads):
            scores = waiting
            if h + 1 < heads:
                waiting = scores_of(h + 1)
            first, second = scores[:rows], scores[rows:]
            old = peaks[h:h + 1, :]
            new = jnp.maximum(
                jnp.where(on_first, jnp.max(first, axis=0, keepdims=True), -INF),
                jnp.where(on_second, jnp.max(second, axis=0, keepdims=True), -INF),
            )
            new = jnp.maximum(old, new)
            e_first = jnp.exp(first - jnp.where(on_first, new, INF))
            e_second = jnp.exp(second - jnp.where(on_second, new, INF))
            keep = jnp.exp(old - new)
            new_peaks.append(new)
            new_totals.append(totals[h:h + 1, :] * keep + jnp.sum(e_first + e_second, axis=0, keepdims=True))
            weights = jnp.concatenate([e_first.astype(jnp.bfloat16), e_second.astype(jnp.bfloat16)], axis=0)
            if pend is not None:
                finish(pend)
            pend = (h, keep, weights)
        finish(pend)
        peak[...] = jnp.concatenate(new_peaks, axis=0)
        total[...] = jnp.concatenate(new_totals, axis=0)

        for after, arrivals in arrive.items():
            @pl.when(slot == after)
            def _(arrivals=arrivals):
                for got, part in arrivals:
                    hop(got, part).wait_recv()
                    for later in route:
                        if route[later][0] == got:
                            hop(later, part).start()
                    hand_over(got, part).start()
        return carry

    lax.fori_loop(0, CHUNKS, chunk, 0)

    gain = out_gain[:, columns]
    pieces = []
    for h in range(heads):
        attended = acc[h * HEAD_DIM:(h + 1) * HEAD_DIM, :] / total[h:h + 1, :]
        mean_sq = jnp.mean(attended * attended, axis=0, keepdims=True)
        pieces.append(attended * lax.rsqrt(mean_sq + 1e-6))
    head_normed = (jnp.concatenate(pieces, axis=0).T * gain).astype(jnp.bfloat16)
    hn[1] = head_normed[rows:]
    swap.start()
    hn[0] = head_normed[:rows]
    loads[4].wait()
    others = pl.ds(pl.multiple_of((1 - core) * half, half), half)
    update = jnp.dot(hn[0], wo[columns, :], preferred_element_type=jnp.float32)
    swap.wait_recv()
    update = update + jnp.dot(hn_in[...], wo[others, :], preferred_element_type=jnp.float32)
    out_ref[...] = (buf[0, 0].astype(jnp.float32) + update).astype(out_ref.dtype)

    for part in parts:
        for slot in route:
            hop(slot, part).wait_send()
        for slot in range(len(route) + 1):
            hand_over(slot, part).wait_send()
    list_copy.wait_send()
    count_copy.wait_send()
    swap.wait_send()


def on_device(tokens, in_gain, w_query, w_key, w_value, w_out, out_gain, covis_list, covis_count):
    views = lax.axis_size("views")
    rows, width = tokens.shape[1:]
    half = width // 2
    slots = len(ring_route(views // 2)[0]) + 1
    slots_listed = covis_list.shape[1]
    hbm = pl.BlockSpec(memory_space=pltpu.HBM)
    vmem = pl.BlockSpec(memory_space=pltpu.VMEM)
    bf16, f32 = jnp.bfloat16, jnp.float32
    heads = half // HEAD_DIM
    dma = pltpu.SemaphoreType.DMA
    out = pl.pallas_call(
        functools.partial(body, views),
        out_shape=jax.ShapeDtypeStruct((rows, width), tokens.dtype),
        in_specs=[hbm] * 9,
        out_specs=vmem,
        scratch_shapes=[
            pltpu.VMEM((slots, 2, rows, width), bf16),
            pltpu.VMEM((width, half), bf16),
            pltpu.VMEM((width, half), bf16),
            pltpu.VMEM((width, half), bf16),
            pltpu.VMEM((width, width), bf16),
            pltpu.VMEM((1, width), f32),
            pltpu.VMEM((1, width), f32),
            pltpu.VMEM((2, 1, slots_listed), jnp.int32),
            pltpu.VMEM((2, 1), jnp.int32),
            pltpu.VMEM((heads, 2 * HEAD_DIM, 2 * rows), bf16),
            pltpu.VMEM((2 * rows, half), bf16),
            pltpu.VMEM((half, 2 * rows), bf16),
            pltpu.VMEM((heads, 2 * rows), f32),
            pltpu.VMEM((heads, 2 * rows), f32),
            pltpu.VMEM((half, 2 * rows), f32),
            pltpu.VMEM((16, 2 * rows), f32),
            pltpu.VMEM((2, rows, half), bf16),
            pltpu.VMEM((rows, half), bf16),
            dma((9,)),
            dma((slots, PARTS)),
            dma((slots, PARTS)),
            dma((slots, PARTS)),
            dma((slots, PARTS)),
            dma((3,)),
            dma((3,)),
        ],
        compiler_params=pltpu.CompilerParams(
            collective_id=0, has_side_effects=True, vmem_limit_bytes=60 * 1024 * 1024
        ),
    )(tokens[0], in_gain[None], w_query, w_key, w_value, w_out, out_gain[None], covis_list, covis_count)
    return out[None]


def solution(mesh):
    in_specs = (
        P(("groups", "views"), None, None),
        P(), P(), P(), P(), P(), P(),
        P(("groups", "views"), None),
        P(("groups", "views")),
    )
    out_specs = P(("groups", "views"), None, None)
    return jax.shard_map(on_device, mesh=mesh, in_specs=in_specs, out_specs=out_specs, check_vma=False)
```

time: 43.7 us -> 36.5 us (0.84)
  Pallas kernels: 41.2 us -> 34 us
    pallas_call x1, Pallas kernels: 41.2 us -> 34 us  [on_device(): pl.pallas_call(functools.partial(body, views), out_shape=jax.ShapeDtypeSt...]
where the time goes in v3:
time: 36.5 us; the launch traced here: 36.3 us
  Pallas kernels  34 us (93%)
  local copies, waits for them, and re-layouts  1.67 us (5%)
  between operations  0.66 us (2%)
    pallas_call x1, Pallas kernels, on_device(): pl.pallas_call(functools.partial(body, views), out_shape=jax.ShapeDtypeSt...  34 us
    unnamed x1, local copies, waits for them, and re-layouts  1.67 us

profile of v3, /device:TPU:1, one launch (start us, length us, event | category | flops | bytes accessed | tf_op | source)
XLA Modules:
  0.0 36.3 jit_solution(953144657320117888)
XLA Ops:
  0.7 34.0 %shard_map.91 = bf16[128,1024]{1,0:T(8,128)(2,1)} custom-call(bf16[128,1024]{1,0:T(8,128)(2,1)} %bitcast.5, f32[1,1024]{1,0:T(1,128)} %bitcast.6, bf16[1024,1024]{1,0:T(8,128)(2,1)} %wq_hbm.1, bf16[1024,1024]{1,0:T(8,128)(2,1)} %wk_hbm.1, bf16[1024,1024]{1,0:T(8,128)(2,1)} %wv_hbm.1, bf16[1024,1024]{1,0:T(8,128)(2,1)} %wo_hbm.1, f32[1,1024]{1,0:T(1,128)} %bitcast.7, ...), custom_call_target="tpu_custom_call" | custom-call | tf_op jit(solution)/shard_map/pallas_call | solution.py:306
  34.7 1.7 %copy.12 = bf16[1,128,1024]{2,1,0:T(8,128)(2,1)} copy(bf16[1,128,1024]{2,1,0:T(8,128)(2,1)} %bitcast.4) | data formatting | bytes 524288
